TPU v7x, 32 devices: a whole 2x2x4 slice. The times are simulated.
32 devices in a mesh: rep: 2 (over y), fsdp: 4 (over z), seq: 4 (over x, core).
Axes of the slice: x: 2, y: 2, z: 4, core: 2. Of those that a mesh axis runs over, the one named last changes fastest.
Arguments:
- latents: bfloat16 [8, 1024, 1152], P(('rep', 'fsdp'), 'seq'), may hold values from -6 to 6
- cond: bfloat16 [8, 1152], P(('rep', 'fsdp')), may hold values from -6 to 6
- w_ada: bfloat16 [1152, 6912], P(('fsdp', 'seq')), may hold values from -0.25 to 0.25
- b_ada: bfloat16 [6912], P(('fsdp', 'seq')), may hold values from -3 to 3
- w_qkv: bfloat16 [1152, 3456], P(('fsdp', 'seq')), may hold values from -0.1875 to 0.1875
- b_qv: bfloat16 [2304], P(('fsdp', 'seq')), may hold values from -3 to 3
- w_out: bfloat16 [1152, 1152], P(('fsdp', 'seq')), may hold values from -1.5 to 1.5
- b_out: bfloat16 [1152], P(('fsdp', 'seq')), may hold values from -3 to 3
- w_one: bfloat16 [1152, 4608], P(('fsdp', 'seq')), may hold values from -0.1875 to 0.1875
- b_one: bfloat16 [4608], P(('fsdp', 'seq')), may hold values from -3 to 3
- w_two: bfloat16 [4608, 1152], P(('fsdp', 'seq')), may hold values from -0.09375 to 0.09375
- b_two: bfloat16 [1152], P(('fsdp', 'seq')), may hold values from -3 to 3
- cotangent: bfloat16 [8, 1024, 1152], P(('rep', 'fsdp'), 'seq'), may hold values from -6 to 6
Outputs:
- block_out: bfloat16 [8, 1024, 1152], P(('rep', 'fsdp'), 'seq')
- grad_latents: float32 [8, 1024, 1152], P(('rep', 'fsdp'), 'seq')
- grad_cond: float32 [8, 1152], P(('rep', 'fsdp'))
- grad_w_ada: float32 [1152, 6912], P(('fsdp', 'seq'))
- grad_b_ada: float32 [6912], P(('fsdp', 'seq'))
- grad_w_qkv: float32 [1152, 3456], P(('fsdp', 'seq'))
- grad_b_qv: float32 [2304], P(('fsdp', 'seq'))
- grad_w_out: float32 [1152, 1152], P(('fsdp', 'seq'))
- grad_b_out: float32 [1152], P(('fsdp', 'seq'))
- grad_w_one: float32 [1152, 4608], P(('fsdp', 'seq'))
- grad_b_one: float32 [4608], P(('fsdp', 'seq'))
- grad_w_two: float32 [4608, 1152], P(('fsdp', 'seq'))
- grad_b_two: float32 [1152], P(('fsdp', 'seq'))
All inputs are finite; a program needn't handle non-finite values.
Results may differ from a plain program's by a relative error of at most 0.014.
The roundings to bfloat16 on the way count: a program that leaves them out, or rounds other values in their place, can miss the bound.
Values may be sent and summed in bfloat16 or wider, within the bound.
A program may use at most 448 MiB of HBM per device.

v0:
```python
import math
import jax
import jax.numpy as jnp
from jax import lax
from jax.sharding import PartitionSpec as P

H = 16
epsilon = 1e-06
gelu_coef = math.sqrt(2.0 / math.pi)


def norm_stats(values):
    center = values - jnp.mean(values, axis=-1, keepdims=True)
    inv_std = lax.rsqrt(jnp.mean(center * center, axis=-1, keepdims=True) + epsilon)
    return (center * inv_std, inv_std)


def norm_back(grad, normed, inv_std):
    return inv_std * (
        grad
        - jnp.mean(grad, axis=-1, keepdims=True)
        - normed * jnp.mean(grad * normed, axis=-1, keepdims=True)
    )


def gelu_tanh(values):
    inner = gelu_coef * (values + 0.044715 * values * values * values)
    return 0.5 * values * (1.0 + jnp.tanh(inner))


def gelu_slope(values):
    inner = gelu_coef * (values + 0.044715 * values * values * values)
    tanh_val = jnp.tanh(inner)
    return 0.5 * (1.0 + tanh_val) + 0.5 * values * (1.0 - tanh_val * tanh_val) * gelu_coef * (
        1.0 + 3.0 * 0.044715 * values * values
    )


def row_dot(left, right):
    return jnp.dot(left, right, preferred_element_type=jnp.float32)


def back_dot(grad, weight):
    return lax.dot_general(
        grad, weight, (((1,), (1,)), ((), ())), preferred_element_type=jnp.float32
    )


def outer_dot(left, grad):
    return lax.dot_general(left, grad, (((0,), (0,)), ((), ())), preferred_element_type=jnp.float32)


def pack_rows(arrays, groups):
    return jnp.concatenate([array.reshape(groups, -1) for array in arrays], axis=1).reshape(-1)


def unpack_rows(flat, layouts, groups):
    pieces = []
    offset = 0
    for layout in layouts:
        amount = math.prod(layout) // groups
        piece = flat[offset : offset + amount].reshape((layout[0] // groups,) + tuple(layout[1:]))
        pieces.append(piece)
        offset = offset + amount
    return pieces


def split_blocks(array, block_len):
    shape = array.shape
    return jnp.moveaxis(
        array.reshape(shape[:2] + (shape[2] // block_len, block_len) + shape[3:]), 2, 0
    )


def join_blocks(array):
    moved = jnp.moveaxis(array, 0, 2)
    shape = moved.shape
    return moved.reshape(shape[:2] + (shape[2] * shape[3],) + shape[4:])


def attention_forward(queries, key_rows, val_rows):
    length = queries.shape[2]
    head_size = queries.shape[3]
    block_len = min(512, length)
    score_scale = head_size ** (-0.5)

    def one_block(query_block):
        scores = (
            jnp.einsum("bhqd,bhkd->bhqk", query_block, key_rows, preferred_element_type=jnp.float32)
            * score_scale
        )
        highest = jnp.max(scores, axis=-1, keepdims=True)
        raised = jnp.exp(scores - highest)
        summed = jnp.sum(raised, axis=-1, keepdims=True)
        probs_low = (raised / summed).astype(jnp.bfloat16)
        result = jnp.einsum(
            "bhqk,bhkd->bhqd", probs_low, val_rows, preferred_element_type=jnp.float32
        )
        return (result.astype(jnp.bfloat16), (highest + jnp.log(summed))[..., 0])

    outputs, log_totals = lax.map(one_block, split_blocks(queries, block_len))
    return (join_blocks(outputs), join_blocks(log_totals))


def attention_backward(queries, key_rows, val_rows, log_totals, grad_out):
    length = queries.shape[2]
    head_size = queries.shape[3]
    block_len = min(512, length)
    score_scale = head_size ** (-0.5)

    def one_block(carried, pieces):
        grad_keys, grad_vals = carried
        query_block, grad_block, lse_block = pieces
        scores = (
            jnp.einsum("bhqd,bhkd->bhqk", query_block, key_rows, preferred_element_type=jnp.float32)
            * score_scale
        )
        attn_probs = jnp.exp(scores - lse_block[..., None])
        grad_probs = jnp.einsum(
            "bhqd,bhkd->bhqk", grad_block, val_rows, preferred_element_type=jnp.float32
        )
        row_inner = jnp.sum(attn_probs * grad_probs, axis=-1, keepdims=True)
        grad_scores = (attn_probs * (grad_probs - row_inner)).astype(jnp.bfloat16)
        grad_query = (
            jnp.einsum("bhqk,bhkd->bhqd", grad_scores, key_rows, preferred_element_type=jnp.float32)
            * score_scale
        )
        grad_keys = (
            grad_keys
            + jnp.einsum(
                "bhqk,bhqd->bhkd", grad_scores, query_block, preferred_element_type=jnp.float32
            )
            * score_scale
        )
        grad_vals = grad_vals + jnp.einsum(
            "bhqk,bhqd->bhkd",
            attn_probs.astype(jnp.bfloat16),
            grad_block,
            preferred_element_type=jnp.float32,
        )
        return ((grad_keys, grad_vals), grad_query)

    zeros_start = jnp.zeros(key_rows.shape, jnp.float32)
    pieces = (
        split_blocks(queries, block_len),
        split_blocks(grad_out, block_len),
        split_blocks(log_totals, block_len),
    )
    (grad_keys, grad_vals), grad_queries = lax.scan(one_block, (zeros_start, zeros_start), pieces)
    return (join_blocks(grad_queries), grad_keys, grad_vals)


def on_device(
    latents, cond, w_ada, b_ada, w_qkv, b_qv, w_out, b_out, w_one, b_one, w_two, b_two, cotangent
):
    latent_count, local_len, width = latents.shape
    token_rows = latent_count * local_len
    head_count = H
    head_size = width // head_count
    seq_count = lax.axis_size("seq")
    group_size = lax.axis_size(("fsdp", "seq"))
    local_heads = head_count // seq_count
    full_len = local_len * seq_count
    owner = lax.axis_index(("fsdp", "seq"))
    own_rows = w_ada.shape[0]
    bias_cols = b_ada.shape[0]
    first_latent = lax.axis_index(("rep", "fsdp")) * latent_count
    cond_float = cond.astype(jnp.float32)
    cond_sigmoid = jax.nn.sigmoid(cond_float)
    silu_cond = (cond_float * cond_sigmoid).astype(jnp.bfloat16)
    silu_every = lax.all_gather(silu_cond, ("rep", "fsdp"), axis=0, tiled=True)
    silu_owned = lax.dynamic_slice_in_dim(silu_every, owner * own_rows, own_rows, 1)
    ada_part = row_dot(silu_owned, w_ada)
    bias_slot = (
        lax.dynamic_slice_in_dim(ada_part, owner * bias_cols, bias_cols, 1)
        + b_ada.astype(jnp.float32)[None, :]
    )
    ada_part = lax.dynamic_update_slice_in_dim(ada_part, bias_slot, owner * bias_cols, 1)
    modulation_every = lax.psum(ada_part, ("fsdp", "seq"))
    modulation = lax.dynamic_slice_in_dim(modulation_every, first_latent, latent_count, 0)
    shift_one, scale_one, gate_one, shift_two, scale_two, gate_two = jnp.split(
        modulation[:, None, :], 6, axis=2
    )
    full_fwd = (
        lax.all_gather(w_qkv, ("fsdp", "seq"), axis=0, tiled=True),
        lax.all_gather(b_qv, ("fsdp", "seq"), axis=0, tiled=True),
        lax.all_gather(w_out, ("fsdp", "seq"), axis=0, tiled=True),
        lax.all_gather(b_out, ("fsdp", "seq"), axis=0, tiled=True),
        lax.all_gather(w_one, ("fsdp", "seq"), axis=0, tiled=True),
        lax.all_gather(b_one, ("fsdp", "seq"), axis=0, tiled=True),
        lax.all_gather(w_two, ("fsdp", "seq"), axis=0, tiled=True),
        lax.all_gather(b_two, ("fsdp", "seq"), axis=0, tiled=True),
    )
    qkv_full, qv_bias, out_full, out_bias, one_full, one_bias, two_full, two_bias = full_fwd
    inputs = latents.astype(jnp.float32)
    normed_one, inv_one = norm_stats(inputs)
    mixed_one = (
        (normed_one * (1.0 + scale_one) + shift_one).astype(jnp.bfloat16).reshape(token_rows, width)
    )
    bias_full = jnp.concatenate(
        [qv_bias[:width], jnp.zeros((width,), jnp.bfloat16), qv_bias[width:]]
    ).astype(jnp.float32)
    projected = (row_dot(mixed_one, qkv_full) + bias_full).astype(jnp.bfloat16)
    token_heads = projected.reshape(latent_count, local_len, 3, head_count, head_size).transpose(
        2, 0, 3, 1, 4
    )
    token_heads = token_heads.reshape(3, latent_count, head_count, local_len * head_size)
    head_tokens = lax.all_to_all(token_heads, "seq", split_axis=2, concat_axis=3, tiled=True)
    head_tokens = head_tokens.reshape(3, latent_count, local_heads, full_len, head_size)
    queries = head_tokens[0]
    key_rows = head_tokens[1]
    val_rows = head_tokens[2]
    attended, log_totals = attention_forward(queries, key_rows, val_rows)
    back_tokens = lax.all_to_all(
        attended.reshape(latent_count, local_heads, full_len * head_size),
        "seq",
        split_axis=2,
        concat_axis=1,
        tiled=True,
    )
    merged = (
        back_tokens.reshape(latent_count, head_count, local_len, head_size)
        .transpose(0, 2, 1, 3)
        .reshape(token_rows, width)
    )
    branch_one = (row_dot(merged, out_full) + out_bias.astype(jnp.float32)).reshape(
        latent_count, local_len, width
    )
    residual = inputs + gate_one * branch_one
    normed_two, inv_two = norm_stats(residual)
    mixed_two = (
        (normed_two * (1.0 + scale_two) + shift_two).astype(jnp.bfloat16).reshape(token_rows, width)
    )
    hidden_pre = row_dot(mixed_two, one_full) + one_bias.astype(jnp.float32)
    hidden_act = gelu_tanh(hidden_pre).astype(jnp.bfloat16)
    branch_two = (row_dot(hidden_act, two_full) + two_bias.astype(jnp.float32)).reshape(
        latent_count, local_len, width
    )
    block_out = (residual + gate_two * branch_two).astype(jnp.bfloat16)
    full_back = (
        lax.all_gather(w_qkv, ("fsdp", "seq"), axis=0, tiled=True),
        lax.all_gather(b_qv, ("fsdp", "seq"), axis=0, tiled=True),
        lax.all_gather(w_out, ("fsdp", "seq"), axis=0, tiled=True),
        lax.all_gather(b_out, ("fsdp", "seq"), axis=0, tiled=True),
        lax.all_gather(w_one, ("fsdp", "seq"), axis=0, tiled=True),
        lax.all_gather(b_one, ("fsdp", "seq"), axis=0, tiled=True),
        lax.all_gather(w_two, ("fsdp", "seq"), axis=0, tiled=True),
        lax.all_gather(b_two, ("fsdp", "seq"), axis=0, tiled=True),
    )
    qkv_back = full_back[0]
    out_back = full_back[2]
    one_back = full_back[4]
    two_back = full_back[6]
    grad_out = cotangent.astype(jnp.float32)
    grad_two = (gate_two * grad_out).astype(jnp.bfloat16).reshape(token_rows, width)
    gate_two_grad = jnp.sum(grad_out * branch_two, axis=1)
    two_w_grad = outer_dot(hidden_act, grad_two)
    two_b_grad = jnp.sum(grad_two, axis=0, dtype=jnp.float32)
    grad_pre = (back_dot(grad_two, two_back) * gelu_slope(hidden_pre)).astype(jnp.bfloat16)
    one_w_grad = outer_dot(mixed_two, grad_pre)
    one_b_grad = jnp.sum(grad_pre, axis=0, dtype=jnp.float32)
    grad_mixed_two = back_dot(grad_pre, one_back).reshape(latent_count, local_len, width)
    shift_two_grad = jnp.sum(grad_mixed_two, axis=1)
    scale_two_grad = jnp.sum(grad_mixed_two * normed_two, axis=1)
    grad_resid = grad_out + norm_back(grad_mixed_two * (1.0 + scale_two), normed_two, inv_two)
    mlp_layouts = (one_w_grad.shape, one_b_grad.shape, two_w_grad.shape, two_b_grad.shape)
    mlp_flat = lax.psum_scatter(
        pack_rows((one_w_grad, one_b_grad, two_w_grad, two_b_grad), group_size),
        ("fsdp", "seq"),
        scatter_dimension=0,
        tiled=True,
    )
    grad_branch = (gate_one * grad_resid).astype(jnp.bfloat16).reshape(token_rows, width)
    gate_one_grad = jnp.sum(grad_resid * branch_one, axis=1)
    out_w_grad = outer_dot(merged, grad_branch)
    out_b_grad = jnp.sum(grad_branch, axis=0, dtype=jnp.float32)
    grad_merged = back_dot(grad_branch, out_back).astype(jnp.bfloat16)
    grad_heads = grad_merged.reshape(latent_count, local_len, head_count, head_size).transpose(
        0, 2, 1, 3
    )
    grad_heads = grad_heads.reshape(latent_count, head_count, local_len * head_size)
    grad_heads = lax.all_to_all(grad_heads, "seq", split_axis=1, concat_axis=2, tiled=True)
    grad_heads = grad_heads.reshape(latent_count, local_heads, full_len, head_size)
    grad_queries, grad_keys, grad_vals = attention_backward(
        queries, key_rows, val_rows, log_totals, grad_heads
    )
    stacked = jnp.stack([grad_queries, grad_keys, grad_vals]).astype(jnp.bfloat16)
    stacked = stacked.reshape(3, latent_count, local_heads, full_len * head_size)
    grad_tokens = lax.all_to_all(stacked, "seq", split_axis=3, concat_axis=2, tiled=True)
    grad_proj = grad_tokens.reshape(3, latent_count, head_count, local_len, head_size).transpose(
        1, 3, 0, 2, 4
    )
    grad_proj = grad_proj.reshape(token_rows, 3 * width)
    qkv_w_grad = outer_dot(mixed_one, grad_proj)
    proj_sums = jnp.sum(grad_proj, axis=0, dtype=jnp.float32)
    qv_b_grad = jnp.concatenate([proj_sums[:width], proj_sums[2 * width :]])
    grad_mixed_one = back_dot(grad_proj, qkv_back).reshape(latent_count, local_len, width)
    shift_one_grad = jnp.sum(grad_mixed_one, axis=1)
    scale_one_grad = jnp.sum(grad_mixed_one * normed_one, axis=1)
    grad_inputs = grad_resid + norm_back(grad_mixed_one * (1.0 + scale_one), normed_one, inv_one)
    partial_mod = jnp.concatenate(
        [
            shift_one_grad,
            scale_one_grad,
            gate_one_grad,
            shift_two_grad,
            scale_two_grad,
            gate_two_grad,
        ],
        axis=1,
    )
    mod_grad = lax.psum(partial_mod, "seq").astype(jnp.bfloat16)
    mod_every = lax.all_gather(mod_grad, ("rep", "fsdp"), axis=0, tiled=True)
    ada_w_grad = outer_dot(silu_owned, mod_every)
    ada_b_grad = jnp.sum(
        lax.dynamic_slice_in_dim(mod_every, owner * bias_cols, bias_cols, 1),
        axis=0,
        dtype=jnp.float32,
    )
    cond_part = back_dot(mod_every, w_ada)
    cond_every = lax.all_gather(cond_part, ("fsdp", "seq"), axis=1, tiled=True)
    cond_lin = lax.dynamic_slice_in_dim(cond_every, first_latent, latent_count, 0)
    cond_grad = cond_lin * cond_sigmoid * (1.0 + cond_float * (1.0 - cond_sigmoid))
    attn_layouts = (qkv_w_grad.shape, qv_b_grad.shape, out_w_grad.shape, out_b_grad.shape)
    attn_flat = lax.psum_scatter(
        pack_rows((qkv_w_grad, qv_b_grad, out_w_grad, out_b_grad), group_size),
        ("fsdp", "seq"),
        scatter_dimension=0,
        tiled=True,
    )
    attn_total, mlp_total = (
        lax.psum(attn_flat.astype(jnp.bfloat16), "rep").astype(jnp.float32),
        lax.psum(mlp_flat.astype(jnp.bfloat16), "rep").astype(jnp.float32),
    )
    attn_parts = unpack_rows(attn_total, attn_layouts, group_size)
    mlp_parts = unpack_rows(mlp_total, mlp_layouts, group_size)
    return (
        block_out,
        grad_inputs,
        cond_grad,
        ada_w_grad,
        ada_b_grad,
        attn_parts[0],
        attn_parts[1],
        attn_parts[2],
        attn_parts[3],
        mlp_parts[0],
        mlp_parts[1],
        mlp_parts[2],
        mlp_parts[3],
    )


def solution(mesh):
    in_specs = (
        P(("rep", "fsdp"), "seq", None),
        P(("rep", "fsdp"), None),
        P(("fsdp", "seq"), None),
        P(("fsdp", "seq")),
        P(("fsdp", "seq"), None),
        P(("fsdp", "seq")),
        P(("fsdp", "seq"), None),
        P(("fsdp", "seq")),
        P(("fsdp", "seq"), None),
        P(("fsdp", "seq")),
        P(("fsdp", "seq"), None),
        P(("fsdp", "seq")),
        P(("rep", "fsdp"), "seq", None),
    )
    out_specs = (
        P(("rep", "fsdp"), "seq", None),
        P(("rep", "fsdp"), "seq", None),
        P(("rep", "fsdp"), None),
        P(("fsdp", "seq"), None),
        P(("fsdp", "seq")),
        P(("fsdp", "seq"), None),
        P(("fsdp", "seq")),
        P(("fsdp", "seq"), None),
        P(("fsdp", "seq")),
        P(("fsdp", "seq"), None),
        P(("fsdp", "seq")),
        P(("fsdp", "seq"), None),
        P(("fsdp", "seq")),
    )
    return jax.shard_map(
        on_device, mesh=mesh, in_specs=in_specs, out_specs=out_specs, check_vma=False
    )
```

profile of v0, /device:TPU:0, one launch (start us, length us, event | category | flops | bytes accessed | tf_op | source)
XLA Modules:
  0.0 3231.1 jit_solution(2037017178745607638)
XLA Ops:
  8.7 32.3 %all-gather = bf16[8,1,1152]{2,1,0:T(2,128)(2,1)S(1)} all-gather(bf16[1,1,1152]{2,1,0:T(2,128)(2,1)S(1)} %get-tuple-element.247), channel_id=1, replica_groups=mesh['rep'=2,'fsdp'=4,'seq'=4] {'rep','fsdp'}, dimensions={0}, use_global_device_ids=true | all-gather | bytes 20736 | tf_op jit(solution)/shard_map/all_gather | solution.py:171
  50.0 57.8 %all-reduce.7 = (bf16[2304]{0:T(1024)(128)(2,1)S(1)}, bf16[1152]{0:T(1024)(128)(2,1)S(1)}, bf16[1152]{0:T(1024)(128)(2,1)S(1)}, bf16[4608]{0:T(1024)(128)(2,1)S(1)}) all-reduce(bf16[2304]{0:T(1024)(128)(2,1)S(1)} %dynamic-update-slice, bf16[1152]{0:T(1024)(128)(2,1)S(1)} %dynamic-update-slice.1, ...), channel_id=1, replica_groups=mesh['rep'=2,'fsdp'=4,'seq'=4] {'fsdp','seq'}, use_global_device_ids=true, to_apply=%add | all-reduce | flops 9216 | bytes 36864
  108.3 25.0 all-reduce.13.cloned.1.call-done
  134.9 73.7 %all-gather.8.cloned.1.call-done = bf16[1152,3456]{1,0:T(8,128)(2,1)} async-done(((bf16[72,3456]{1,0:T(8,128)(2,1)}), bf16[1152,3456]{1,0:T(8,128)(2,1)}) %all-gather.8.cloned.1.call-update) | async-done | bytes 7962640 | tf_op jit(solution)/shard_map/all_gather | solution.py:185
  233.5 35.5 %all-to-all-done = bf16[3,1,16,18432]{3,0,1,2:T(4,128)(2,1)S(1)} async-done(((bf16[3,1,16,18432]{3,0,1,2:T(4,128)(2,1)}), bf16[3,1,16,18432]{3,0,1,2:T(4,128)(2,1)S(1)}, u32[]{:S(2)}, u32[]{:S(2)}) %all-to-all-start) | async-done | bytes 1769504 | tf_op jit(solution)/shard_map/all_to_all | solution.py:208
  299.4 56.5 %copy.113 = bf16[1,4,73728]{1,0,2:T(2,128)(2,1)} copy(bf16[1,4,73728]{2,1,0:T(4,128)(2,1)S(1)} %reshape_reshape.6) | data formatting | bytes 1179648 | tf_op jit(solution)/shard_map/reshape;reshape | solution.py:215
  356.5 400.0 %reduce.40 = bf16[73728,4]{1,0:T(8,128)(2,1)} reduce(bf16[73728,1,4]{2,1,0:T(2,128)(2,1)} %bitcast.242, bf16[]{:T(256)} %broadcast.232), dimensions={1}, to_apply=%bitcast.165.reduce_sub_computation | reduce | bytes 1179650
  756.5 51.0 %reshape.503 = bf16[4,2,36864]{2,1,0:T(2,128)(2,1)} reshape(bf16[73728,4]{1,0:T(8,128)(2,1)} %reduce.40) | data formatting | bytes 1179648
  821.7 61.7 %reshape.504 = bf16[73728,1,4]{2,1,0:T(2,128)(2,1)} reshape(bf16[4,2,36864]{2,1,0:T(2,128)(2,1)} %all-to-all-done.1) | data formatting | bytes 1179648
  883.4 69.2 %copy.114 = bf16[1,4,73728]{2,1,0:T(4,128)(2,1)} copy(bf16[1,4,73728]{1,0,2:T(2,128)(2,1)} %bitcast.243) | data formatting | bytes 1179648 | tf_op jit(solution)/shard_map/all_to_all | solution.py:214
  1041.6 19.7 reshape.451
  1105.1 38.5 %while.28 = (s32[]{:T(128)}, f32[1,4,1024,72]{2,3,1,0:T(8,128)}, f32[1,4,1024,72]{2,3,1,0:T(8,128)S(1)}, bf16[2,1,4,512,72]{3,4,2,1,0:T(8,128)(2,1)}, bf16[2,1,4...) while((s32[]{:T(128)}, f32[1,4,1024,72]{2,3,1,0:T(8,128)}, ...), condition=%wide.region_13.14_spmd.clone, body=%wide.region_11.13_spmd.clone.sunk | while | flops 1536735232 | bytes 133357912 | solution.py:149
  1159.2 70.1 %copy.128 = bf16[3,1,4,73728]{2,0,1,3:T(4,128)(2,1)} copy(bf16[3,1,4,73728]{3,2,1,0:T(4,128)(2,1)S(1)} %pad_maximum_fusion) | data formatting | bytes 3538944 | tf_op jit(solution)/shard_map/stack | solution.py:287
  1229.2 89.9 %reshape.507 = bf16[4,2,110592]{2,1,0:T(2,128)(2,1)} reshape(bf16[73728,1,3,4]{3,2,1,0:T(4,128)(2,1)} %bitcast.169) | data formatting | bytes 3538944
  1336.6 19.7 reshape.453
  1357.8 57.9 %dynamic-update-slice.6 = f32[16,663912]{1,0:T(8,128)} dynamic-update-slice(f32[16,663912]{1,0:T(8,128)} %dynamic-update-slice.5, f32[16,331776]{1,0:T(8,128)} %reshape.453, s32[]{} %constant.143, s32[]{} %constant.145) | dynamic-update-slice | bytes 42467332
  1417.2 56.3 %reshape.455 = f32[10622592]{0:T(1024)} reshape(f32[16,663912]{1,0:T(8,128)} %dynamic-update-slice.7) | data formatting | bytes 84980736 | tf_op jit(solution)/shard_map/reshape | solution.py:54
  1473.5 102.3 %reshape.508 = bf16[73728,1,3,4]{3,2,1,0:T(4,128)(2,1)} reshape(bf16[4,2,110592]{2,1,0:T(2,128)(2,1)S(1)} %all-to-all-done.3) | data formatting | bytes 3538944
  1575.8 101.6 %copy.134 = bf16[3,1,4,4,18432]{4,3,2,0,1:T(4,128)(2,1)} copy(bf16[3,1,4,4,18432]{2,0,4,3,1:T(4,128)(2,1)} %bitcast.33) | data formatting | bytes 3538944 | tf_op jit(solution)/shard_map/all_to_all | solution.py:289
  1755.2 26.6 reshape.448
  1781.8 1341.9 %all-reduce.16 = (bf16[5311872]{0:T(1024)(128)(2,1)}, bf16[10622592]{0:T(1024)(128)(2,1)}) all-reduce(f32[5311872]{0:T(1024)} %reshape.448, f32[10622592]{0:T(1024)} %reshape.455), channel_id=2, replica_groups=mesh['rep'=2,'fsdp'=4,'seq'=4] {'fsdp','seq'}, use_global_device_ids=true, to_apply=%region_26.27.clone | all-reduce | flops 15934464 | bytes 95606784
  3132.6 22.9 psum.29
  3155.6 31.3 all-gather.1
  3187.2 18.8 all-gather.2
  (308 shorter events, 401.8 us)
Async XLA Ops:
  7.2 41.8 %copy-start.53 = (bf16[72]{0:T(256)(128)(2,1)S(1)}, bf16[72]{0:T(256)(128)(2,1)}, u32[]{:S(2)}) copy-start(bf16[72]{0:T(256)(128)(2,1)} %param.24) | copy-start | bytes 436
  7.2 42.0 %copy-start.54 = (bf16[72]{0:T(256)(128)(2,1)S(1)}, bf16[72]{0:T(256)(128)(2,1)}, u32[]{:S(2)}) copy-start(bf16[72]{0:T(256)(128)(2,1)} %param.28) | copy-start | bytes 436
  7.2 42.3 %copy-start.55 = (bf16[144]{0:T(256)(128)(2,1)S(1)}, bf16[144]{0:T(256)(128)(2,1)}, u32[]{:S(2)}) copy-start(bf16[144]{0:T(256)(128)(2,1)} %param.22) | copy-start | bytes 868
  7.2 42.5 %copy-start.52 = (bf16[288]{0:T(512)(128)(2,1)S(1)}, bf16[288]{0:T(512)(128)(2,1)}, u32[]{:S(2)}) copy-start(bf16[288]{0:T(512)(128)(2,1)} %param.26) | copy-start | bytes 1732
  7.2 100.5 %copy-start.10 = (bf16[1,256,1152]{2,1,0:T(8,128)(2,1)S(1)}, bf16[1,256,1152]{2,1,0:T(8,128)(2,1)}, u32[]{:S(2)}) copy-start(bf16[1,256,1152]{2,1,0:T(8,128)(2,1)} %param.17) | copy-start | bytes 1769476
  7.3 126.1 %all-reduce.13.cloned.1.call-start = ((), (), s32[]{:S(2)}) async-start(), calls=%async_computation.4 | async-start | bytes 442368 | tf_op jit(solution)/shard_map/psum | solution.py:179
  43.8 164.9 %all-gather.8.cloned.1.call-start = ((), (), s32[]{:S(2)}) async-start(), calls=%async_computation.5 | async-start | bytes 8460288 | tf_op jit(solution)/shard_map/all_gather | solution.py:185
  44.5 919.2 %all-gather.10.cloned.1.call-start = ((), (), s32[]{:S(2)}) async-start(), calls=%async_computation.6 | async-start | bytes 2820096 | tf_op jit(solution)/shard_map/all_gather | solution.py:187
  45.2 923.9 %all-gather.12.cloned.1.call-start = ((), (), s32[]{:S(2)}) async-start(), calls=%async_computation.7 | async-start | bytes 11280384 | tf_op jit(solution)/shard_map/all_gather | solution.py:189
  45.8 933.3 %all-gather.14.cloned.1.call-start = ((), (), s32[]{:S(2)}) async-start(), calls=%async_computation.8 | async-start | bytes 11280384 | tf_op jit(solution)/shard_map/all_gather | solution.py:191
  108.0 100.7 %copy-start.38 = (f32[256]{0:T(256)}, f32[256]{0:T(256)S(1)}, u32[]{:S(2)}) copy-start(f32[256]{0:T(256)S(1)} %broadcast_multiply_fusion.5) | copy-start | bytes 3076
  108.3 100.4 %copy-start.42 = (f32[256]{0:T(256)}, f32[256]{0:T(256)S(1)}, u32[]{:S(2)}) copy-start(f32[256]{0:T(256)S(1)} %add_rsqrt_fusion.1) | copy-start | bytes 3076
  134.9 73.7 %copy-start.27 = (f32[1152]{0:T(1024)}, f32[1152]{0:T(1024)S(1)}, u32[]{:S(2)}) copy-start(f32[1152]{0:T(1024)S(1)} %get-tuple-element.202) | copy-start | bytes 13828
  134.9 73.7 %copy-start.30 = (f32[1152]{0:T(1024)}, f32[1152]{0:T(1024)S(1)}, u32[]{:S(2)}) copy-start(f32[1152]{0:T(1024)S(1)} %get-tuple-element.201) | copy-start | bytes 13828
  229.4 39.6 %all-to-all-start = ((bf16[3,1,16,18432]{3,0,1,2:T(4,128)(2,1)}), bf16[3,1,16,18432]{3,0,1,2:T(4,128)(2,1)S(1)}, u32[]{:S(2)}, u32[]{:S(2)}) async-start(bf16[3,1,16,18432]{3,0,1,2:T(4,128)(2,1)} %reshape.492), calls=%async_computation | async-start | bytes 4718592 | tf_op jit(solution)/shard_map/all_to_all | solution.py:208
  294.9 61.0 %copy-start.4 = (bf16[1,4,1024,72]{2,3,1,0:T(8,128)(2,1)}, bf16[1,4,1024,72]{2,3,1,0:T(8,128)(2,1)S(1)}, u32[]{:S(2)}) copy-start(bf16[1,4,1024,72]{2,3,1,0:T(8,128)(2,1)S(1)} %get-tuple-element.443) | copy-start | bytes 1769476
  294.9 61.0 %copy-start.33 = (f32[2,1,4,512]{3,2,1,0:T(4,128)}, f32[2,1,4,512]{3,2,1,0:T(4,128)S(1)}, u32[]{:S(2)}) copy-start(f32[2,1,4,512]{3,2,1,0:T(4,128)S(1)} %get-tuple-element.405) | copy-start | bytes 49156
  807.5 14.2 all-to-all-start.1
  1037.0 48.5 %all-to-all-start.2 = ((bf16[4,2,36864]{2,1,0:T(2,128)(2,1)}), bf16[4,2,36864]{2,1,0:T(2,128)(2,1)}, u32[]{:S(2)}, u32[]{:S(2)}) async-start(bf16[4,2,36864]{2,1,0:T(2,128)(2,1)} %reshape.505), calls=%async_computation.2 | async-start | bytes 1179648 | tf_op jit(solution)/shard_map/all_to_all | solution.py:282
  1319.1 154.4 %all-to-all-start.3 = ((bf16[4,2,110592]{2,1,0:T(2,128)(2,1)}), bf16[4,2,110592]{2,1,0:T(2,128)(2,1)S(1)}, u32[]{:S(2)}, u32[]{:S(2)}) async-start(bf16[4,2,110592]{2,1,0:T(2,128)(2,1)} %reshape.507), calls=%async_computation.3 | async-start | bytes 3538944 | tf_op jit(solution)/shard_map/all_to_all | solution.py:289
  1322.9 1886.3 %all-reduce.15.cloned.1.call-start = ((), (), s32[]{:S(2)}) async-start(), calls=%async_computation.9 | async-start | bytes 3989504 | tf_op jit(solution)/shard_map/psum | solution.py:332
  3129.3 77.6 %copy-start.47 = (bf16[8,1,72]{2,1,0:T(2,128)(2,1)S(1)}, bf16[8,1,72]{2,1,0:T(2,128)(2,1)}, u32[]{:S(2)}) copy-start(bf16[8,1,72]{2,1,0:T(2,128)(2,1)} %copy-done.46) | copy-start | bytes 3460
  3132.5 76.1 %copy-start.44 = (bf16[1,1152]{1,0:T(2,128)(2,1)S(1)}, bf16[1,1152]{1,0:T(2,128)(2,1)}, u32[]{:S(2)}) copy-start(bf16[1,1152]{1,0:T(2,128)(2,1)} %param.18) | copy-start | bytes 6916
  3132.5 76.1 %copy-start.45 = (f32[1,1152]{1,0:T(1,128)S(1)}, f32[1,1152]{1,0:T(1,128)}, u32[]{:S(2)}) copy-start(f32[1,1152]{1,0:T(1,128)} %get-tuple-element.248) | copy-start | bytes 13828
  (49 other events, 322.6 us)
Sparse Core Ops, SparseCore 0:
  43.9 89.4 all-reduce.12
  135.5 73.1 all-gather.7
  210.8 48.3 all-gather.9
  261.4 87.6 all-gather.11
  351.2 86.8 all-gather.13
  3129.4 68.6 all-reduce.14
where the time goes:
time: 3250 us; the launch traced here: 3230 us
  blocking collectives  1510 us (46%)
  local copies, waits for them, and re-layouts  984 us (30%)
  other arithmetic  434 us (13%)
  waiting for transfers between devices  145 us (4%)
  matrix products  128 us (4%)
    unnamed x2, blocking collectives  1400 us
    unnamed x127, local copies, waits for them, and re-layouts  428 us
    unnamed x5, other arithmetic  407 us
    all_to_all x2, local copies, waits for them, and re-layouts, on_device(): lax.all_to_all(stacked, 'seq', split_axis=3, concat_axis=2, tiled=True)  104 us
    reshape x2, local copies, waits for them, and re-layouts, pack_rows(): jnp.concatenate([array.reshape(groups, -1) for array in arrays], axis=1)  82.9 us
    another operation x4, local copies, waits for them, and re-layouts, on_device(): jnp.stack([grad_queries, grad_keys, grad_vals]).astype(jnp.bfloat16)  78 us
    all_to_all x3, local copies, waits for them, and re-layouts, on_device(): lax.all_to_all(attended.reshape(latent_count, local_heads, full_len * hea...  73.9 us
    all_gather x1, waiting for transfers between devices, on_device(): lax.all_gather(w_qkv, ('fsdp', 'seq'), axis=0, tiled=True)  73.7 us
  transfers between devices with their start and end apart: 10, of which 4 were waited for; matrix products, arithmetic and copies ran while one was open for 28% of the time, Pallas kernels for 0%

commit v1 on v0

--- a/solution.py
+++ b/solution.py
@@ -286,7 +286,10 @@
     )
     stacked = jnp.stack([grad_queries, grad_keys, grad_vals]).astype(jnp.bfloat16)
     stacked = stacked.reshape(3, latent_count, local_heads, full_len * head_size)
-    grad_tokens = lax.all_to_all(stacked, "seq", split_axis=3, concat_axis=2, tiled=True)
+    grad_tokens = jnp.concatenate(
+        lax.all_to_all(jnp.stack(jnp.split(stacked, lax.axis_size("seq"), axis=3)), "seq", 0, 0),
+        axis=2,
+    )
     grad_proj = grad_tokens.reshape(3, latent_count, head_count, local_len, head_size).transpose(
         1, 3, 0, 2, 4
     )

time: 3250 us -> 2890 us (0.89)
  local copies, waits for them, and re-layouts: 984 us -> 629 us
    unnamed x127 -> x123, local copies, waits for them, and re-layouts: 428 us -> 239 us
    all_to_all x2 -> x0, local copies, waits for them, and re-layouts: 104 us -> none  [on_device(): lax.all_to_all(stacked, 'seq', split_axis=3, concat_axis=2, tiled=True)]
    another operation x4, local copies, waits for them, and re-layouts: 78 us -> 9.38 us  [on_device(): jnp.stack([grad_queries, grad_keys, grad_vals]).astype(jnp.bfloat16)]
  transfers between devices with their start and end apart: 10 -> 10, of which waited for: 4 -> 4; matrix products, arithmetic and copies ran while one was open for 28% -> 32% of each run, Pallas kernels for 0% -> 0%
where the time goes in v1:
time: 2890 us; the launch traced here: 2880 us
  blocking collectives  1500 us (52%)
  local copies, waits for them, and re-layouts  629 us (22%)
  other arithmetic  434 us (15%)
  waiting for transfers between devices  145 us (5%)
  matrix products  128 us (4%)
    unnamed x2, blocking collectives  1400 us
    unnamed x5, other arithmetic  407 us
    unnamed x123, local copies, waits for them, and re-layouts  239 us
    reshape x2, local copies, waits for them, and re-layouts, pack_rows(): jnp.concatenate([array.reshape(groups, -1) for array in arrays], axis=1)  83.1 us
    all_to_all x3, local copies, waits for them, and re-layouts, on_device(): lax.all_to_all(attended.reshape(latent_count, local_heads, full_len * hea...  73.9 us
    all_gather x1, waiting for transfers between devices, on_device(): lax.all_gather(w_qkv, ('fsdp', 'seq'), axis=0, tiled=True)  73.7 us
    reshape x7, local copies, waits for them, and re-layouts, pack_rows(): array.reshape(groups, -1)  59.9 us
    another operation x2, local copies, waits for them, and re-layouts, on_device(): attended.reshape(latent_count, local_heads, full_len * head_size)  59.5 us
  transfers between devices with their start and end apart: 10, of which 4 were waited for; matrix products, arithmetic and copies ran while one was open for 32% of the time, Pallas kernels for 0%

profile of v1, /device:TPU:0, one launch (start us, length us, event | category | flops | bytes accessed | tf_op | source)
XLA Modules:
  0.0 2877.0 jit_solution(979329752042765566)
XLA Ops:
  8.6 32.3 %all-gather = bf16[8,1,1152]{2,1,0:T(2,128)(2,1)S(1)} all-gather(bf16[1,1,1152]{2,1,0:T(2,128)(2,1)S(1)} %get-tuple-element.232), channel_id=1, replica_groups=mesh['rep'=2,'fsdp'=4,'seq'=4] {'rep','fsdp'}, dimensions={0}, use_global_device_ids=true | all-gather | bytes 20736 | tf_op jit(solution)/shard_map/all_gather | solution.py:171
  50.0 57.8 %all-reduce.7 = (bf16[2304]{0:T(1024)(128)(2,1)S(1)}, bf16[1152]{0:T(1024)(128)(2,1)S(1)}, bf16[1152]{0:T(1024)(128)(2,1)S(1)}, bf16[4608]{0:T(1024)(128)(2,1)S(1)}) all-reduce(bf16[2304]{0:T(1024)(128)(2,1)S(1)} %dynamic-update-slice, bf16[1152]{0:T(1024)(128)(2,1)S(1)} %dynamic-update-slice.1, ...), channel_id=1, replica_groups=mesh['rep'=2,'fsdp'=4,'seq'=4] {'fsdp','seq'}, use_global_device_ids=true, to_apply=%add | all-reduce | flops 9216 | bytes 36864
  108.2 25.0 all-reduce.13.cloned.1.call-done
  134.9 73.7 %all-gather.8.cloned.1.call-done = bf16[1152,3456]{1,0:T(8,128)(2,1)} async-done(((bf16[72,3456]{1,0:T(8,128)(2,1)}), bf16[1152,3456]{1,0:T(8,128)(2,1)}) %all-gather.8.cloned.1.call-update) | async-done | bytes 7962640 | tf_op jit(solution)/shard_map/all_gather | solution.py:185
  233.3 35.5 %all-to-all-done = bf16[3,1,16,18432]{3,0,1,2:T(4,128)(2,1)S(1)} async-done(((bf16[3,1,16,18432]{3,0,1,2:T(4,128)(2,1)}), bf16[3,1,16,18432]{3,0,1,2:T(4,128)(2,1)S(1)}, u32[]{:S(2)}, u32[]{:S(2)}) %all-to-all-start) | async-done | bytes 1769504 | tf_op jit(solution)/shard_map/all_to_all | solution.py:208
  299.4 56.5 %copy.92 = bf16[1,4,73728]{1,0,2:T(2,128)(2,1)} copy(bf16[1,4,73728]{2,1,0:T(4,128)(2,1)S(1)} %reshape_reshape.9) | data formatting | bytes 1179648 | tf_op jit(solution)/shard_map/reshape;reshape | solution.py:215
  356.5 400.0 %reduce.40 = bf16[73728,4]{1,0:T(8,128)(2,1)} reduce(bf16[73728,1,4]{2,1,0:T(2,128)(2,1)} %bitcast.250, bf16[]{:T(256)} %broadcast.232), dimensions={1}, to_apply=%bitcast.175.reduce_sub_computation | reduce | bytes 1179650
  756.5 51.0 %reshape.502 = bf16[4,2,36864]{2,1,0:T(2,128)(2,1)} reshape(bf16[73728,4]{1,0:T(8,128)(2,1)} %reduce.40) | data formatting | bytes 1179648
  821.5 61.7 %reshape.503 = bf16[73728,1,4]{2,1,0:T(2,128)(2,1)} reshape(bf16[4,2,36864]{2,1,0:T(2,128)(2,1)} %all-to-all-done.1) | data formatting | bytes 1179648
  883.2 69.2 %copy.93 = bf16[1,4,73728]{2,1,0:T(4,128)(2,1)} copy(bf16[1,4,73728]{1,0,2:T(2,128)(2,1)} %bitcast.251) | data formatting | bytes 1179648 | tf_op jit(solution)/shard_map/all_to_all | solution.py:214
  1041.3 19.7 reshape.450
  1061.0 15.2 constant_dynamic-update-slice_fusion.10
  1104.5 38.9 %while.28 = (s32[]{:T(128)}, f32[1,4,1024,72]{2,3,1,0:T(8,128)}, f32[1,4,1024,72]{2,3,1,0:T(8,128)S(1)}, bf16[2,1,4,512,72]{3,4,2,1,0:T(8,128)(2,1)}, bf16[2,1,4...) while((s32[]{:T(128)}, f32[1,4,1024,72]{2,3,1,0:T(8,128)}, ...), condition=%wide.region_13.14_spmd.clone, body=%wide.region_11.13_spmd.clone.sunk | while | flops 1536735232 | bytes 133357912 | solution.py:149
  1172.5 13.7 fusion.77
  1186.2 19.7 reshape.452
  1207.5 57.9 %dynamic-update-slice.6 = f32[16,663912]{1,0:T(8,128)} dynamic-update-slice(f32[16,663912]{1,0:T(8,128)} %dynamic-update-slice.5, f32[16,331776]{1,0:T(8,128)} %reshape.452, s32[]{} %constant.143, s32[]{} %constant.145) | dynamic-update-slice | bytes 42467332
  1266.9 56.4 %reshape.454 = f32[10622592]{0:T(1024)} reshape(f32[16,663912]{1,0:T(8,128)} %dynamic-update-slice.7) | data formatting | bytes 84980736 | tf_op jit(solution)/shard_map/reshape | solution.py:54
  1355.6 15.2 reshape.444
  1383.3 16.0 dynamic-update-slice.10
  1400.8 26.6 reshape.447
  1427.5 1341.9 %all-reduce.16 = (bf16[5311872]{0:T(1024)(128)(2,1)}, bf16[10622592]{0:T(1024)(128)(2,1)}) all-reduce(f32[5311872]{0:T(1024)} %reshape.447, f32[10622592]{0:T(1024)} %reshape.454), channel_id=2, replica_groups=mesh['rep'=2,'fsdp'=4,'seq'=4] {'fsdp','seq'}, use_global_device_ids=true, to_apply=%region_26.27.clone | all-reduce | flops 15934464 | bytes 95606784
  2778.3 22.9 psum.29
  2801.2 31.3 %all-gather.1 = bf16[8,1,6912]{2,1,0:T(2,128)(2,1)S(1)} all-gather(bf16[1,1,6912]{2,1,0:T(2,128)(2,1)S(1)} %bitcast.271), channel_id=1, replica_groups=mesh['rep'=2,'fsdp'=4,'seq'=4] {'rep','fsdp'}, dimensions={0}, use_global_device_ids=true | all-gather | bytes 124416 | tf_op jit(solution)/shard_map/all_gather | solution.py:316
  2832.9 18.8 all-gather.2
  (305 shorter events, 350.9 us)
Async XLA Ops:
  7.2 35.1 %copy-start = (bf16[72,6912]{1,0:T(8,128)(2,1)S(1)}, bf16[72,6912]{1,0:T(8,128)(2,1)}, u32[]{:S(2)}) copy-start(bf16[72,6912]{1,0:T(8,128)(2,1)} %param.19) | copy-start | bytes 2985988
  7.2 126.1 %all-reduce.13.cloned.1.call-start = ((), (), s32[]{:S(2)}) async-start(), calls=%async_computation.4 | async-start | bytes 442368 | tf_op jit(solution)/shard_map/psum | solution.py:179
  42.3 65.4 %copy-start.10 = (bf16[1,256,1152]{2,1,0:T(8,128)(2,1)S(1)}, bf16[1,256,1152]{2,1,0:T(8,128)(2,1)}, u32[]{:S(2)}) copy-start(bf16[1,256,1152]{2,1,0:T(8,128)(2,1)} %param.17) | copy-start | bytes 1769476
  43.7 164.9 %all-gather.8.cloned.1.call-start = ((), (), s32[]{:S(2)}) async-start(), calls=%async_computation.5 | async-start | bytes 8460288 | tf_op jit(solution)/shard_map/all_gather | solution.py:185
  44.5 919.2 %all-gather.10.cloned.1.call-start = ((), (), s32[]{:S(2)}) async-start(), calls=%async_computation.6 | async-start | bytes 2820096 | tf_op jit(solution)/shard_map/all_gather | solution.py:187
  45.2 924.0 %all-gather.12.cloned.1.call-start = ((), (), s32[]{:S(2)}) async-start(), calls=%async_computation.7 | async-start | bytes 11280384 | tf_op jit(solution)/shard_map/all_gather | solution.py:189
  45.8 933.3 %all-gather.14.cloned.1.call-start = ((), (), s32[]{:S(2)}) async-start(), calls=%async_computation.8 | async-start | bytes 11280384 | tf_op jit(solution)/shard_map/all_gather | solution.py:191
  107.9 100.7 %copy-start.36 = (f32[256]{0:T(256)}, f32[256]{0:T(256)S(1)}, u32[]{:S(2)}) copy-start(f32[256]{0:T(256)S(1)} %broadcast_multiply_fusion.5) | copy-start | bytes 3076
  108.2 100.4 %copy-start.40 = (f32[256]{0:T(256)}, f32[256]{0:T(256)S(1)}, u32[]{:S(2)}) copy-start(f32[256]{0:T(256)S(1)} %add_rsqrt_fusion.1) | copy-start | bytes 3076
  134.9 73.7 %copy-start.27 = (f32[1152]{0:T(1024)}, f32[1152]{0:T(1024)S(1)}, u32[]{:S(2)}) copy-start(f32[1152]{0:T(1024)S(1)} %get-tuple-element.187) | copy-start | bytes 13828
  134.9 73.7 %copy-start.30 = (f32[1152]{0:T(1024)}, f32[1152]{0:T(1024)S(1)}, u32[]{:S(2)}) copy-start(f32[1152]{0:T(1024)S(1)} %get-tuple-element.186) | copy-start | bytes 13828
  229.4 39.4 %all-to-all-start = ((bf16[3,1,16,18432]{3,0,1,2:T(4,128)(2,1)}), bf16[3,1,16,18432]{3,0,1,2:T(4,128)(2,1)S(1)}, u32[]{:S(2)}, u32[]{:S(2)}) async-start(bf16[3,1,16,18432]{3,0,1,2:T(4,128)(2,1)} %reshape.491), calls=%async_computation | async-start | bytes 4718592 | tf_op jit(solution)/shard_map/all_to_all | solution.py:208
  294.7 61.3 %copy-start.4 = (bf16[1,4,1024,72]{2,3,1,0:T(8,128)(2,1)}, bf16[1,4,1024,72]{2,3,1,0:T(8,128)(2,1)S(1)}, u32[]{:S(2)}) copy-start(bf16[1,4,1024,72]{2,3,1,0:T(8,128)(2,1)S(1)} %get-tuple-element.431) | copy-start | bytes 1769476
  294.7 61.3 %copy-start.33 = (f32[2,1,4,512]{3,2,1,0:T(4,128)}, f32[2,1,4,512]{3,2,1,0:T(4,128)S(1)}, u32[]{:S(2)}) copy-start(f32[2,1,4,512]{3,2,1,0:T(4,128)S(1)} %get-tuple-element.393) | copy-start | bytes 49156
  807.5 14.0 all-to-all-start.1
  1037.0 47.9 %all-to-all-start.2 = ((bf16[4,2,36864]{2,1,0:T(2,128)(2,1)}), bf16[4,2,36864]{2,1,0:T(2,128)(2,1)}, u32[]{:S(2)}, u32[]{:S(2)}) async-start(bf16[4,2,36864]{2,1,0:T(2,128)(2,1)} %reshape.504), calls=%async_computation.2 | async-start | bytes 1179648 | tf_op jit(solution)/shard_map/all_to_all | solution.py:282
  1061.0 15.2 copy-start.21
  1168.7 154.6 %all-to-all-start.3 = ((bf16[4,3,1,4,18432]{4,3,1,2,0:T(4,128)(2,1)}), bf16[4,3,1,4,18432]{4,3,1,2,0:T(4,128)(2,1)S(1)}, u32[]{:S(2)}, u32[]{:S(2)}) async-start(bf16[4,3,1,4,18432]{4,3,1,2,0:T(4,128)(2,1)} %pad_maximum_fusion), calls=%async_computation.3 | async-start | bytes 3538944 | tf_op jit(solution)/shard_map/all_to_all | solution.py:290
  1172.4 1682.4 %all-reduce.15.cloned.1.call-start = ((), (), s32[]{:S(2)}) async-start(), calls=%async_computation.9 | async-start | bytes 3989504 | tf_op jit(solution)/shard_map/psum | solution.py:335
  1186.2 19.7 copy-start.38
  1383.3 16.0 copy-start.39
  2778.2 74.3 %copy-start.45 = (bf16[8,1,72]{2,1,0:T(2,128)(2,1)S(1)}, bf16[8,1,72]{2,1,0:T(2,128)(2,1)}, u32[]{:S(2)}) copy-start(bf16[8,1,72]{2,1,0:T(2,128)(2,1)} %copy-done.44) | copy-start | bytes 3460
  2832.5 21.7 copy-start.42
  2832.5 21.7 copy-start.43
  (47 other events, 201.3 us)
Sparse Core Ops, SparseCore 0:
  43.8 89.4 all-reduce.12
  135.5 73.1 all-gather.7
  210.8 48.3 all-gather.9
  261.4 87.5 all-gather.11
  351.1 86.8 all-gather.13
  2775.1 68.6 all-reduce.14
